TPU v7x, 32 devices: a whole 2x2x4 slice. The times are simulated.
32 devices in a mesh: leaf: 8 (over z, x), row: 2 (over y), col: 2 (over core).
Axes of the slice: x: 2, y: 2, z: 4, core: 2. Of those that a mesh axis runs over, the one named last changes fastest.
Arguments:
- leaf_rhs: bfloat16 [8, 4096, 128], P('leaf', ('row', 'col')), may hold values from -6 to 6
- leaf_factor: bfloat16 [8, 4096, 4096], P('leaf', ('row', 'col')), as said below
- leaf_coupling: bfloat16 [8, 4096, 4096], P('leaf', None, ('row', 'col')), may hold values from -0.046875 to 0.046875
- border_rows: int32 [8, 4096], P('leaf'), may hold values from 0 to 4095, as said below
- border_count: int32 [8], P('leaf'), may hold values from 1024 to 4096, as said below
- separator_rhs: bfloat16 [4096, 128], P(('leaf', 'row', 'col')), may hold values from -6 to 6
- separator_factor: bfloat16 [4096, 4096], P(('leaf', 'row', 'col')), as said below
Outputs:
- leaf_solution: float32 [8, 4096, 128], P('leaf', ('row', 'col'))
- separator_solution: float32 [4096, 128], P(('leaf', 'row', 'col'))
Inputs may be any that keep to these rules, and one draw needn't show every extreme that they name: `border_rows`: the 4096 row numbers of one section are distinct. Border rows j < border_count[k] of section k are live, the others are unused; some section has all 4096 live. `leaf_factor`: lower triangular with a positive diagonal. `separator_factor`: lower triangular with a positive diagonal.
All inputs are finite; a program needn't handle non-finite values.
Results may differ from a plain program's by a relative error of at most 0.013.
Values may be sent and summed in bfloat16 or wider, within the bound.
No kernel may reach another device: no remote copies, remote signals or barrier semaphores. Data moves between devices by JAX's collectives and lax.ppermute only.
A program may use at most 64 MiB of HBM per device.

v0:
```python
import jax
import jax.numpy as jnp
from jax import lax
from jax.sharding import PartitionSpec as P


def local(
    leaf_rhs, leaf_factor, leaf_coupling, border_rows, border_count, separator_rhs, separator_factor
):
    contract_first = (((0,), (0,)), ((), ()))
    rhs_local = leaf_rhs[0]
    factor_local = leaf_factor[0]
    coupling = leaf_coupling[0]
    index_set = border_rows[0]
    live = jnp.arange(index_set.shape[0], dtype=jnp.int32) < border_count[0]
    columns = rhs_local.shape[1]
    block = factor_local
    forward = jnp.dot(
        block,
        lax.all_gather(rhs_local, ("row", "col"), axis=0, tiled=True),
        preferred_element_type=jnp.float32,
    ).astype(jnp.bfloat16)
    update = jnp.dot(coupling, forward, preferred_element_type=jnp.float32)
    update = jnp.where(live[:, None], update, 0.0)
    sep_rows = separator_factor.shape[0]
    sep_order = separator_factor.shape[1]
    position = lax.axis_index(("leaf", "row", "col")) * sep_rows
    placed = lax.dynamic_update_slice_in_dim(
        jnp.zeros((sep_order, columns), jnp.float32), separator_rhs.astype(jnp.float32), position, 0
    )
    placed = placed.at[index_set].add(-update)
    whole = lax.psum(placed, ("leaf", "row", "col")).astype(jnp.bfloat16)
    root_forward = jnp.dot(separator_factor, whole, preferred_element_type=jnp.float32).astype(
        jnp.bfloat16
    )
    partial_terms = lax.dot_general(
        separator_factor, root_forward, contract_first, preferred_element_type=jnp.float32
    )
    totals = lax.psum(partial_terms, ("leaf", "row", "col"))
    separator_solution = lax.dynamic_slice_in_dim(totals, position, sep_rows, 0)
    rounded = totals.astype(jnp.bfloat16)
    border = jnp.where(live[:, None], rounded[index_set], jnp.zeros((), jnp.bfloat16))
    corrected = (
        forward.astype(jnp.float32)
        - lax.dot_general(coupling, border, contract_first, preferred_element_type=jnp.float32)
    ).astype(jnp.bfloat16)
    block = factor_local
    solution = lax.psum_scatter(
        lax.dot_general(
            block, corrected, contract_first, preferred_element_type=jnp.float32
        ).astype(jnp.bfloat16),
        ("row", "col"),
        scatter_dimension=0,
        tiled=True,
    ).astype(jnp.float32)
    return (solution[None], separator_solution)


def solution(mesh):
    placed = (
        P("leaf", ("row", "col"), None),
        P("leaf", ("row", "col"), None),
        P("leaf", None, ("row", "col")),
        P("leaf", None),
        P("leaf"),
        P(("leaf", "row", "col"), None),
        P(("leaf", "row", "col"), None),
    )
    return jax.shard_map(
        local,
        mesh=mesh,
        in_specs=placed,
        out_specs=(P("leaf", ("row", "col"), None), P(("leaf", "row", "col"), None)),
        check_vma=False,
    )
```

profile of v0, /device:TPU:0, one launch (start us, length us, event | category | flops | bytes accessed | tf_op | source)
XLA Modules:
  0.0 322.0 jit_solution(7589405319605890312)
XLA Ops:
  7.2 0.0 copy-start
  7.2 0.0 copy-start.2
  7.2 0.0 copy-start.3
  7.2 0.0 all-gather.3.cloned.1.call-start
  7.2 0.7 all-gather.3.cloned.1.call-update
  7.9 0.0 all-reduce.3.cloned.1.call-start
  8.6 0.1 broadcast_in_dim.38
  8.8 0.0 copy-done.2
  8.8 0.0 copy-done.3
  8.9 20.2 %all-gather.3.cloned.1.call-done = bf16[1,4096,128]{2,1,0:T(8,128)(2,1)} async-done(((bf16[1,1024,128]{2,1,0:T(8,128)(2,1)}), bf16[1,4096,128]{2,1,0:T(8,128)(2,1)}) %all-gather.3.cloned.1.call-update) | async-done | bytes 1048592 | tf_op jit(solution)/shard_map/all_gather | solution.py:20
  29.0 0.0 copy-start.1
  29.0 6.1 %fusion.32 = bf16[1024,128]{1,0:T(8,128)(2,1)S(1)} fusion(bf16[1,1024,4096]{2,1,0:T(8,128)(2,1)} %param.8, bf16[1,4096,128]{2,1,0:T(8,128)(2,1)} %all-gather.3.cloned.1.call-done), kind=kOutput, calls=%fused_computation.19 | convolution fusion | flops 1073872896 | bytes 9699328 | tf_op jit(solution)/shard_map/dot_general | solution.py:18
  35.1 0.0 copy-done.1
  35.1 4.4 %fusion.17 = f32[4096,128]{1,0:T(8,128)} fusion(bf16[1024,128]{1,0:T(8,128)(2,1)S(1)} %fusion.32, bf16[1,4096,1024]{2,1,0:T(8,128)(2,1)S(1)} %copy-done.1, pred[4096]{0:T(1024)(128)(4,1)S(1)} %iota_compare_fusion), kind=kOutput, calls=%fused_computation.14 | convolution fusion | flops 1074790400 | bytes 10752000 | tf_op jit(solution)/shard_map/dot_general | solution.py:23
  39.5 23.4 %scatter_fusion = f32[4096,128]{1,0:T(8,128)S(1)} fusion(f32[4096,128]{1,0:T(8,128)S(1)} %convert_dynamic-update-slice_fusion, s32[4096]{0:T(1024)S(1)} %bitcast.59, f32[4096,128]{1,0:T(8,128)} %fusion.17), kind=kCustom, calls=%fused_computation.1 | custom fusion | flops 524288 | bytes 6307840 | tf_op jit(solution)/shard_map/scatter-add | solution.py:31
  63.0 62.4 %all-reduce.4 = bf16[4096,128]{1,0:T(8,128)(2,1)} all-reduce(f32[4096,128]{1,0:T(8,128)S(1)} %scatter_fusion), channel_id=1, replica_groups=mesh['leaf'=8,'row'=2,'col'=2] {'leaf','row','col'}, use_global_device_ids=true, to_apply=%region_1.2 | all-reduce | flops 524288 | bytes 3145728 | tf_op jit(solution)/shard_map/psum | solution.py:32
  125.3 0.0 copy-done
  125.3 3.9 %convolution_bitcast_fusion = f32[4096,128]{0,1:T(8,128)} fusion(bf16[128,4096]{1,0:T(8,128)(2,1)S(1)} %copy-done, bf16[4096,128]{1,0:T(8,128)(2,1)} %all-reduce.4), kind=kOutput, calls=%fused_computation.10 | convolution fusion | flops 268451840 | bytes 4194304 | tf_op jit(solution)/shard_map/dot_general | solution.py:36
  129.2 0.0 all-reduce.3.cloned.1.call-update
  129.2 0.2 reduce-scatter.2.cloned.1.call-start
  129.5 133.4 %all-reduce.3.cloned.1.call-done = f32[4096,128]{0,1:T(8,128)} async-done(((f32[4096,128]{0,1:T(8,128)}), f32[4096,128]{0,1:T(8,128)}) %all-reduce.3.cloned.1.call-update) | async-done | bytes 2097168 | tf_op jit(solution)/shard_map/psum | solution.py:39
  262.8 1.7 convert_element_type.34
  264.6 0.7 copy.12
  265.2 12.1 %gather_fusion = bf16[4096,128]{1,0:T(8,128)(2,1)S(1)} fusion(bf16[4096,128]{1,0:T(8,128)(2,1)S(1)} %copy.12, s32[4096]{0:T(1024)S(1)} %broadcast_clamp_fusion), kind=kCustom, calls=%fused_computation | custom fusion | bytes 2113536 | tf_op jit(solution)/shard_map/gather | solution.py:42
  277.4 12.4 %fusion.20 = bf16[4096,128]{0,1:T(8,128)(2,1)} fusion(bf16[1,1024,4096]{2,1,0:T(8,128)(2,1)} %param.8, bf16[1,4096,1024]{2,1,0:T(8,128)(2,1)} %param.9, bf16[4096,128]{1,0:T(8,128)(2,1)S(1)} %gather_fusion, pred[4096]{0:T(1024)(128)(4,1)S(1)} %iota_compare_fusion, bf16[1024,128]{1,0:T(8,128)(2,1)S(1)} %fusion.32), kind=kOutput, calls=%fused_computation.15 | convolution fusion | flops 2148925440 | bytes 19140608 | tf_op jit(solution)/shard_map/dot_general | solution.py:49
  289.8 0.0 reduce-scatter.2.cloned.1.call-update
  289.8 0.9 constant_dynamic-slice_fusion
  290.6 0.7 copy.14
  291.4 22.1 %reduce-scatter.2.cloned.1.call-done = bf16[1024,128]{0,1:T(8,128)(2,1)} async-done(((bf16[4096,128]{0,1:T(8,128)(2,1)}), bf16[1024,128]{0,1:T(8,128)(2,1)}) %reduce-scatter.2.cloned.1.call-update) | async-done | bytes 262160 | tf_op jit(solution)/shard_map/reduce_scatter | solution.py:48
  313.5 1.0 bitcast_convert_fusion
  314.5 1.0 copy.13
  (4 shorter events, 0.0 us)
Async XLA Ops:
  7.2 118.2 %copy-start = (bf16[128,4096]{1,0:T(8,128)(2,1)S(1)}, bf16[128,4096]{1,0:T(8,128)(2,1)}, u32[]{:S(2)}) copy-start(bf16[128,4096]{1,0:T(8,128)(2,1)} %param.13) | copy-start | bytes 3145732
  7.2 1.6 copy-start.2
  7.2 1.6 copy-start.3
  7.2 21.8 %all-gather.3.cloned.1.call-start = ((), (), s32[]{:S(2)}) async-start(), calls=%async_computation.3 | async-start | bytes 1310720 | tf_op jit(solution)/shard_map/all_gather | solution.py:20
  7.9 254.9 %all-reduce.3.cloned.1.call-start = ((), (), s32[]{:S(2)}) async-start(), calls=%async_computation.1 | async-start | bytes 4194304 | tf_op jit(solution)/shard_map/psum | solution.py:39
  29.0 6.1 %copy-start.1 = (bf16[1,4096,1024]{2,1,0:T(8,128)(2,1)S(1)}, bf16[1,4096,1024]{2,1,0:T(8,128)(2,1)}, u32[]{:S(2)}) copy-start(bf16[1,4096,1024]{2,1,0:T(8,128)(2,1)} %param.9) | copy-start | bytes 25165828
  129.2 184.3 %reduce-scatter.2.cloned.1.call-start = ((), (), s32[]{:S(2)}) async-start(), calls=%async_computation.2 | async-start | bytes 1310720 | tf_op jit(solution)/shard_map/reduce_scatter | solution.py:48
Sparse Core Ops, SparseCore 0:
  9.6 19.4 all-gather.2
  129.4 133.4 all-reduce.2
  289.9 23.5 reduce-scatter.1
where the time goes:
time: 322 us
  waiting for transfers between devices  176 us (55%)
  blocking collectives  62.4 us (19%)
  matrix products  26.7 us (8%)
  other arithmetic  26.2 us (8%)
  local copies, waits for them, and re-layouts  15.5 us (5%)
  between operations  14.5 us (5%)
    psum x1, waiting for transfers between devices, local(): totals = lax.psum(partial_terms, ('leaf', 'row', 'col'))  133 us
    psum x1, blocking collectives, local(): whole = lax.psum(placed, ('leaf', 'row', 'col')).astype(jnp.bfloat16)  62.4 us
    scatter-add x1, other arithmetic, local(): placed = placed.at[index_set].add(-update)  23.4 us
    reduce_scatter x1, waiting for transfers between devices, local(): lax.psum_scatter(lax.dot_general(block, corrected, contract_first, prefer...  22.1 us
    all_gather x1, waiting for transfers between devices, local(): lax.all_gather(rhs_local, ('row', 'col'), axis=0, tiled=True)  20.2 us
    dot_general x1, matrix products, local(): lax.dot_general(block, corrected, contract_first, preferred_element_type=...  12.4 us
    gather x1, local copies, waits for them, and re-layouts, local(): rounded[index_set]  12.1 us
  transfers between devices with their start and end apart: 3, of which 3 were waited for; matrix products, arithmetic and copies ran while one was open for 1% of the time, Pallas kernels for 0%

commit v1 on v0

--- a/solution.py
+++ b/solution.py
@@ -29,7 +29,7 @@
         jnp.zeros((sep_order, columns), jnp.float32), separator_rhs.astype(jnp.float32), position, 0
     )
     placed = placed.at[index_set].add(-update)
-    whole = lax.psum(placed, ("leaf", "row", "col")).astype(jnp.bfloat16)
+    whole = lax.psum(lax.psum(placed, ("row", "col")), "leaf").astype(jnp.bfloat16)
     root_forward = jnp.dot(separator_factor, whole, preferred_element_type=jnp.float32).astype(
         jnp.bfloat16
     )

time: 322 us -> 404 us (1.25)
  waiting for transfers between devices: 176 us -> 228 us
  blocking collectives: 62.4 us -> 93 us
    psum x0 -> x1, waiting for transfers between devices: none -> 51.5 us  [local(): lax.psum(placed, ('row', 'col'))]
    psum x1, blocking collectives: 62.4 us -> 93 us  [local(): lax.psum(lax.psum(placed, ('row', 'col')), 'leaf').astype(jnp.bfloat16)]
  transfers between devices with their start and end apart: 3 -> 4, of which waited for: 3 -> 4; matrix products, arithmetic and copies ran while one was open for 1% -> 0% of each run, Pallas kernels for 0% -> 0%
where the time goes in v1:
time: 404 us
  waiting for transfers between devices  228 us (56%)
  blocking collectives  93 us (23%)
  other arithmetic  26.2 us (6%)
  matrix products  25.5 us (6%)
  local copies, waits for them, and re-layouts  16.8 us (4%)
  between operations  14.6 us (4%)
    psum x1, waiting for transfers between devices, local(): totals = lax.psum(partial_terms, ('leaf', 'row', 'col'))  133 us
    psum x1, blocking collectives, local(): lax.psum(lax.psum(placed, ('row', 'col')), 'leaf').astype(jnp.bfloat16)  93 us
    psum x1, waiting for transfers between devices, local(): lax.psum(placed, ('row', 'col'))  51.5 us
    scatter-add x1, other arithmetic, local(): placed = placed.at[index_set].add(-update)  23.4 us
    reduce_scatter x1, waiting for transfers between devices, local(): lax.psum_scatter(lax.dot_general(block, corrected, contract_first, prefer...  22.1 us
    all_gather x1, waiting for transfers between devices, local(): lax.all_gather(rhs_local, ('row', 'col'), axis=0, tiled=True)  20.2 us
    dot_general x1, matrix products, local(): lax.dot_general(block, corrected, contract_first, preferred_element_type=...  12.4 us
    gather x1, local copies, waits for them, and re-layouts, local(): rounded[index_set]  12.1 us
  transfers between devices with their start and end apart: 4, of which 4 were waited for; matrix products, arithmetic and copies ran while one was open for 0% of the time, Pallas kernels for 0%

profile of v1, /device:TPU:0, one launch (start us, length us, event | category | flops | bytes accessed | tf_op | source)
XLA Modules:
  0.0 404.0 jit_solution(7059633886408595267)
XLA Ops:
  7.2 0.0 copy-start
  7.2 0.0 copy-start.3
  7.2 0.0 copy-start.4
  7.2 0.0 all-gather.3.cloned.1.call-start
  7.2 0.7 all-gather.3.cloned.1.call-update
  7.9 0.0 all-reduce.4.cloned.1.call-start
  8.6 0.1 broadcast_in_dim.38
  8.8 0.0 copy-done.4
  8.9 20.2 %all-gather.3.cloned.1.call-done = bf16[1,4096,128]{2,1,0:T(8,128)(2,1)} async-done(((bf16[1,1024,128]{2,1,0:T(8,128)(2,1)}), bf16[1,4096,128]{2,1,0:T(8,128)(2,1)}) %all-gather.3.cloned.1.call-update) | async-done | bytes 1048592 | tf_op jit(solution)/shard_map/all_gather | solution.py:20
  29.0 6.1 %fusion.32 = bf16[1024,128]{1,0:T(8,128)(2,1)S(1)} fusion(bf16[1,1024,4096]{2,1,0:T(8,128)(2,1)} %param.8, bf16[1,4096,128]{2,1,0:T(8,128)(2,1)} %all-gather.3.cloned.1.call-done), kind=kOutput, calls=%fused_computation.19 | convolution fusion | flops 1073872896 | bytes 9699328 | tf_op jit(solution)/shard_map/dot_general | solution.py:18
  35.1 0.0 copy-done.2
  35.1 4.4 %fusion.17 = f32[4096,128]{1,0:T(8,128)} fusion(bf16[1024,128]{1,0:T(8,128)(2,1)S(1)} %fusion.32, bf16[1,4096,1024]{2,1,0:T(8,128)(2,1)S(1)} %copy-done.2, pred[4096]{0:T(1024)(128)(4,1)S(1)} %iota_compare_fusion), kind=kOutput, calls=%fused_computation.14 | convolution fusion | flops 1074790400 | bytes 10752000 | tf_op jit(solution)/shard_map/dot_general | solution.py:23
  39.5 23.4 %scatter_fusion = f32[4096,128]{1,0:T(8,128)S(1)} fusion(f32[4096,128]{1,0:T(8,128)S(1)} %convert_dynamic-update-slice_fusion, s32[4096]{0:T(1024)S(1)} %bitcast.59, f32[4096,128]{1,0:T(8,128)} %fusion.17), kind=kCustom, calls=%fused_computation.1 | custom fusion | flops 524288 | bytes 6307840 | tf_op jit(solution)/shard_map/scatter-add | solution.py:31
  63.0 1.3 copy-done.1
  64.3 0.0 all-reduce.4.cloned.1.call-update
  64.3 0.0 all-reduce.6.cloned.1.call-start
  64.4 51.5 %all-reduce.4.cloned.1.call-done = f32[4096,128]{1,0:T(8,128)} async-done(((f32[4096,128]{1,0:T(8,128)}), f32[4096,128]{1,0:T(8,128)}) %all-reduce.4.cloned.1.call-update) | async-done | bytes 2097168 | tf_op jit(solution)/shard_map/psum | solution.py:32
  115.8 93.0 %all-reduce.7 = bf16[4096,128]{1,0:T(8,128)(2,1)S(1)} all-reduce(f32[4096,128]{1,0:T(8,128)} %all-reduce.4.cloned.1.call-done), channel_id=1, replica_groups=mesh['leaf'=8,'row'=2,'col'=2] {'leaf'}, use_global_device_ids=true, to_apply=%region_2.3 | all-reduce | flops 524288 | bytes 3145728 | tf_op jit(solution)/shard_map/psum | solution.py:32
  208.8 2.6 convolution_bitcast_fusion
  211.5 0.0 all-reduce.6.cloned.1.call-update
  211.5 0.2 reduce-scatter.2.cloned.1.call-start
  211.8 133.0 %all-reduce.6.cloned.1.call-done = f32[4096,128]{0,1:T(8,128)} async-done(((f32[4096,128]{0,1:T(8,128)}), f32[4096,128]{0,1:T(8,128)}) %all-reduce.6.cloned.1.call-update) | async-done | bytes 2097168 | tf_op jit(solution)/shard_map/psum | solution.py:39
  344.8 1.7 convert_element_type.34
  346.5 0.7 copy.12
  347.2 12.1 %gather_fusion = bf16[4096,128]{1,0:T(8,128)(2,1)S(1)} fusion(bf16[4096,128]{1,0:T(8,128)(2,1)S(1)} %copy.12, s32[4096]{0:T(1024)S(1)} %broadcast_clamp_fusion), kind=kCustom, calls=%fused_computation | custom fusion | bytes 2113536 | tf_op jit(solution)/shard_map/gather | solution.py:42
  359.3 12.4 %fusion.20 = bf16[4096,128]{0,1:T(8,128)(2,1)} fusion(bf16[1,1024,4096]{2,1,0:T(8,128)(2,1)} %param.8, bf16[1,4096,1024]{2,1,0:T(8,128)(2,1)} %param.9, bf16[4096,128]{1,0:T(8,128)(2,1)S(1)} %gather_fusion, pred[4096]{0:T(1024)(128)(4,1)S(1)} %iota_compare_fusion, bf16[1024,128]{1,0:T(8,128)(2,1)S(1)} %fusion.32), kind=kOutput, calls=%fused_computation.15 | convolution fusion | flops 2148925440 | bytes 19140608 | tf_op jit(solution)/shard_map/dot_general | solution.py:49
  371.7 0.0 reduce-scatter.2.cloned.1.call-update
  371.8 0.9 constant_dynamic-slice_fusion
  372.6 0.7 copy.14
  373.3 22.1 %reduce-scatter.2.cloned.1.call-done = bf16[1024,128]{0,1:T(8,128)(2,1)} async-done(((bf16[4096,128]{0,1:T(8,128)(2,1)}), bf16[1024,128]{0,1:T(8,128)(2,1)}) %reduce-scatter.2.cloned.1.call-update) | async-done | bytes 262160 | tf_op jit(solution)/shard_map/reduce_scatter | solution.py:48
  395.5 1.0 bitcast_convert_fusion
  396.5 1.0 copy.13
  (8 shorter events, 0.1 us)
Async XLA Ops:
  7.2 201.7 %copy-start = (bf16[128,4096]{1,0:T(8,128)(2,1)S(1)}, bf16[128,4096]{1,0:T(8,128)(2,1)}, u32[]{:S(2)}) copy-start(bf16[128,4096]{1,0:T(8,128)(2,1)} %param.13) | copy-start | bytes 3145732
  7.2 1.6 copy-start.3
  7.2 1.6 copy-start.4
  7.2 21.8 %all-gather.3.cloned.1.call-start = ((), (), s32[]{:S(2)}) async-start(), calls=%async_computation.4 | async-start | bytes 1310720 | tf_op jit(solution)/shard_map/all_gather | solution.py:20
  7.9 107.9 %all-reduce.4.cloned.1.call-start = ((), (), s32[]{:S(2)}) async-start(), calls=%async_computation.1 | async-start | bytes 4194304 | tf_op jit(solution)/shard_map/psum | solution.py:32
  29.0 6.1 %copy-start.2 = (bf16[1,4096,1024]{2,1,0:T(8,128)(2,1)S(1)}, bf16[1,4096,1024]{2,1,0:T(8,128)(2,1)}, u32[]{:S(2)}) copy-start(bf16[1,4096,1024]{2,1,0:T(8,128)(2,1)} %param.9) | copy-start | bytes 25165828
  63.0 1.3 copy-start.1
  64.3 280.5 %all-reduce.6.cloned.1.call-start = ((), (), s32[]{:S(2)}) async-start(), calls=%async_computation.2 | async-start | bytes 4194304 | tf_op jit(solution)/shard_map/psum | solution.py:39
  211.5 184.0 %reduce-scatter.2.cloned.1.call-start = ((), (), s32[]{:S(2)}) async-start(), calls=%async_computation.3 | async-start | bytes 1310720 | tf_op jit(solution)/shard_map/reduce_scatter | solution.py:48
Sparse Core Ops, SparseCore 0:
  9.6 19.4 all-gather.2
  64.4 51.3 all-reduce.3
  211.6 133.1 all-reduce.5
  371.9 23.5 reduce-scatter.1
